TPU v7x, 32 devices: a whole 2x2x4 slice. The times are simulated.
32 devices in a mesh: row: 8 (over z, core), col: 4 (over y, x).
Axes of the slice: x: 2, y: 2, z: 4, core: 2. Of those that a mesh axis runs over, the one named last changes fastest.
Arguments:
- density: bfloat16 [8192, 8192], P('row', 'col'), may hold values from -6 to 6
- listed: int32 [64, 64], P('row', 'col'), may hold values 0 or 1
- three_centre: bfloat16 [128, 512, 512], P(('row', 'col')), may hold values from -0.25 to 0.25
Outputs:
- exchange_diag: float32 [8192, 512], P('row', 'col')
- exchange_density: bfloat16 [8192, 8192], P('row', 'col')
All inputs are finite; a program needn't handle non-finite values. No bound on the sum of `listed` on one device may be relied on, other than what follows from the above.
Results may differ from a plain program's by a relative error of at most 0.0058.
Values may be sent and summed in bfloat16 or wider, within the bound.
A program may use at most 64 MiB of HBM per device.

v0:
```python
import functools

import jax
import jax.numpy as jnp
from jax import lax
from jax.experimental import pallas as pl
from jax.experimental.pallas import tpu as pltpu
from jax.sharding import PartitionSpec as P

TILE = 128
W = 512
SUP = W // TILE
UNIT = W // 2
PART = UNIT // 2
PIECE = 32
BAND = 512
MESH = pl.DeviceIdType.MESH


def from_root(value, axis, root):
    mine = lax.axis_index(axis) == root
    return lax.psum(jnp.where(mine, value, jnp.zeros_like(value)), axis)


def partner_2(block, axis, stride):
    count = lax.axis_size(axis)
    route = []
    for low in range(count):
        high = low | 1 << stride
        if high != low and high < count:
            route += [(low, high), (high, low)]
    return lax.ppermute(block, axis, route)


def halve_rows(values, row_index, levels, sender):
    for bit_level in reversed(range(levels)):
        middle = values.shape[0] // 2
        lower_half = row_index // 2**bit_level % 2 == 0
        kept_rows = jnp.where(lower_half, values[:middle], values[middle:])
        sent_rows = jnp.where(lower_half, values[middle:], values[:middle])
        values = kept_rows + sender(sent_rows, bit_level)
    return values


def per_device(density, listed, three_centre):
    tile_rows = listed.shape[0]
    tile_cols = listed.shape[1]
    quad_tiles = max(tile_rows, 4)
    groups_dev = quad_tiles // 4
    aux_count = three_centre.shape[0]
    col_count = lax.axis_size("col")
    row_index = lax.axis_index("row")
    col_index = lax.axis_index("col")
    masked = (
        density.reshape(tile_rows, TILE, tile_cols, TILE)
        * listed[:, None, :, None].astype(jnp.bfloat16)
    ).reshape(tile_rows * TILE, tile_cols * TILE)
    quad_start = row_index * tile_rows // quad_tiles * quad_tiles
    col_offset = quad_start % tile_cols * TILE
    portion = lax.dynamic_slice_in_dim(masked, col_offset, quad_tiles * TILE, 1)
    diagonal = from_root(portion, "col", quad_start // tile_cols)
    joined = jnp.concatenate([diagonal, masked], axis=1)
    levels = (quad_tiles // tile_rows).bit_length() - 1
    for bit_level in range(levels):
        partner = partner_2(joined, "row", bit_level)
        lower_half = row_index // 2**bit_level % 2 == 0
        joined = jnp.where(
            lower_half,
            jnp.concatenate([joined, partner], axis=0),
            jnp.concatenate([partner, joined], axis=0),
        )
    quad_block = joined[:, : quad_tiles * TILE]
    quad_density = joined[:, quad_tiles * TILE :]
    group_ids = jnp.arange(groups_dev, dtype=jnp.int32)
    exchange_quad = jnp.zeros((groups_dev, W, W), jnp.float32)
    for aux_slot in range(aux_count):
        group_slot = (col_index * aux_count + aux_slot) % groups_dev
        density_sub = lax.dynamic_slice(quad_block, (group_slot * W, group_slot * W), (W, W))
        aux_block = three_centre[aux_slot]
        half_product = jnp.dot(aux_block, density_sub, preferred_element_type=jnp.float32).astype(
            jnp.bfloat16
        )
        contribution = lax.dot_general(
            half_product, aux_block, (((1,), (1,)), ((), ())), preferred_element_type=jnp.float32
        )
        exchange_quad = exchange_quad + jnp.where(
            (group_ids == group_slot)[:, None, None], contribution[None], 0.0
        )
    aux_group = aux_count * col_count * 4 // tile_rows
    exchange_quad = (exchange_quad * aux_group ** (-0.5)).reshape(quad_tiles * TILE, W)
    column_share = lax.psum_scatter(exchange_quad, "col", scatter_dimension=1, tiled=True)
    exchange_diag = halve_rows(
        column_share,
        row_index,
        levels,
        lambda sent_rows, bit_level: partner_2(sent_rows, "row", bit_level),
    )
    fock_rounded = lax.all_gather(exchange_diag.astype(jnp.bfloat16), "col", axis=1, tiled=True)
    rows_here = tile_rows * TILE
    segment_rows = min(rows_here, W)
    segment_count = rows_here // segment_rows
    within_quad = (row_index * tile_rows - quad_start) * TILE
    products = []
    for segment in range(segment_count):
        group_position = (within_quad + segment * segment_rows) // W
        dens_rows = lax.dynamic_slice_in_dim(quad_density, group_position * W, W, 0)
        fock_part = fock_rounded[segment * segment_rows : (segment + 1) * segment_rows]
        products.append(
            jnp.dot(fock_part, dens_rows, preferred_element_type=jnp.float32) * W ** (-0.5)
        )
    exchange_density = jnp.concatenate(products, axis=0).astype(jnp.bfloat16)
    return (exchange_diag, exchange_density)


def mask_tile(tile, flag):
    return tile * jnp.full(tile.shape, flag.astype(jnp.float32)).astype(jnp.bfloat16)


def exchange_kernel(
    scale, listed, density, three_centre, diag_out, fock_out,
    raw, block, coef, half, partial, send_1, recv_1, send_2, recv_2, diag, fock,
    raw_sem, coef_sem, diag_sem, fock_sem, bc_send, bc_recv, rs1_send, rs1_recv,
    rs2_send, rs2_recv, ag1_send, ag1_recv, ag2_send, ag2_recv,
):
    tile_rows, tile_cols = listed.shape
    groups = tile_rows // SUP
    units = groups * (W // UNIT)
    aux_count = three_centre.shape[0]
    row = lax.axis_index("row")
    me = lax.axis_index("col")
    x, y = me % 2, me // 2
    xn, yn = me + 1 - 2 * x, me + 2 - 4 * y
    far = xn + yn - me
    near = (xn, yn)
    first_tile = row * tile_rows
    owner = first_tile // tile_cols
    tile_off = first_tile % tile_cols
    ox, oy = owner % 2, owner // 2
    rx, ry = (x + ox) % 2, (y + oy) % 2
    even = (rx + ry + 1) % 2
    is_owner = rx + ry == 0
    hop_to = (xn * even + yn * (1 - even), yn * even + xn * (1 - even))
    last_of = (rx + 2 * (1 - ry) == 0, ry + 2 * (1 - rx) == 0)
    relays_of = (
        (rx + ry) * (rx + 1 - ry) > 0,
        (rx + ry) * (ry + 1 - rx) > 0,
    )

    def remote(src, dst, send_sem, recv_sem, target):
        return pltpu.make_async_remote_copy(
            src_ref=src, dst_ref=dst, send_sem=send_sem, recv_sem=recv_sem,
            device_id=(row, target), device_id_type=MESH,
        )

    def raw_copy(g):
        columns = pl.ds(pl.multiple_of((tile_off + g * SUP) * TILE, TILE), W)
        return pltpu.make_async_copy(
            density.at[pl.ds(g * W, W), columns], raw.at[g], raw_sem.at[g]
        )

    def coef_copy(q):
        return pltpu.make_async_copy(three_centre.at[q], coef.at[q], coef_sem.at[q])

    per_path = W // PIECE // 2

    def piece(g, i):
        part = block.at[g, pl.ds(i * PIECE, PIECE)]
        return remote(part, part, bc_send.at[g, i], bc_recv.at[g, i], hop_to[i // per_path])

    @pl.when(is_owner)
    def _():
        for g in range(groups):
            raw_copy(g).start()

    barrier = pltpu.get_barrier_semaphore()
    for neighbour in near:
        pl.semaphore_signal(barrier, inc=1, device_id=(row, neighbour), device_id_type=MESH)
    for q in range(aux_count):
        coef_copy(q).start()
    pl.semaphore_wait(barrier, 2)

    order = [s + h * per_path for s in range(per_path) for h in range(2)]

    @pl.when(is_owner)
    def _():
        for g in range(groups):
            raw_copy(g).wait()
            for i in order:
                rows = pl.ds(i * PIECE, PIECE)
                for j in range(SUP):
                    cols = pl.ds(j * TILE, TILE)
                    flag = listed[g * SUP + i * PIECE // TILE, tile_off + g * SUP + j]
                    block[g, rows, cols] = mask_tile(raw[g, rows, cols], flag)
                piece(g, i).start()

    def relay(g, pieces):
        for i in pieces:
            @pl.when(relays_of[i // per_path])
            def _():
                piece(g, i).wait_recv()
                piece(g, i).start()

    def stage_1(u, h):
        return remote(send_1.at[u, h], recv_1.at[u, h], rs1_send.at[u, h], rs1_recv.at[u, h], near[h])

    def stage_2(u, h):
        return remote(
            send_2.at[u, h], recv_2.at[u, h], rs2_send.at[u, h], rs2_recv.at[u, h], near[1 - h]
        )

    def columns_of(dev):
        return pl.ds(pl.multiple_of(dev * TILE, TILE), TILE)

    def rows_of(u, h):
        return pl.ds(u * UNIT + h * PART, PART)

    def gather_1(u, axis):
        part = fock.at[pl.ds(u * UNIT, UNIT), columns_of(me)]
        return remote(part, part, ag1_send.at[u, axis], ag1_recv.at[u, axis], near[axis])

    def gather_2(u, axis):
        part = fock.at[rows_of(u, axis), columns_of(near[1 - axis])]
        return remote(part, part, ag2_send.at[u, axis], ag2_recv.at[u, axis], near[axis])

    def diag_copy(u):
        rows = pl.ds(u * UNIT, UNIT)
        return pltpu.make_async_copy(diag.at[rows], diag_out.at[rows], diag_sem.at[u])

    def fock_copy(u):
        rows = pl.ds(u * UNIT, UNIT)
        return pltpu.make_async_copy(fock.at[rows], fock_out.at[rows], fock_sem.at[u])

    for g in range(groups):
        relay(g, order)
    for q in range(aux_count):
        coef_copy(q).wait()
    for g in range(groups):
        members = list(range(g, aux_count, groups))
        for h in range(2):
            @pl.when(last_of[h])
            def _():
                for s in range(per_path):
                    piece(g, s + h * per_path).wait_recv()
        for n, q in enumerate(members):
            half[n] = jnp.dot(coef[q], block[g], preferred_element_type=jnp.float32).astype(jnp.bfloat16)
        for v in range(W // UNIT):
            u = g * (W // UNIT) + v
            rows = pl.ds(v * UNIT, UNIT)
            for n, q in enumerate(members):
                term = lax.dot_general(
                    half[n, rows], coef[q], (((1,), (1,)), ((), ())),
                    preferred_element_type=jnp.float32,
                )
                if n == 0:
                    partial[pl.ds(u * UNIT, UNIT)] = term
                else:
                    partial[pl.ds(u * UNIT, UNIT)] += term
            for h in range(2):
                send_1[u, h, 0] = partial[rows_of(u, h), columns_of(near[h])].astype(jnp.bfloat16)
                send_1[u, h, 1] = partial[rows_of(u, h), columns_of(far)].astype(jnp.bfloat16)
                stage_1(u, h).start()

    for phase, step in [(p, u) for p in range(4) for u in range(units)]:
        if phase == 0:
            u = step
            for h in range(2):
                stage_1(u, h).wait_recv()
                send_2[u, h] = (
                    partial[rows_of(u, h), columns_of(near[1 - h])]
                    + recv_1[u, h, 1].astype(jnp.float32)
                ).astype(jnp.bfloat16)
                stage_2(u, h).start()
        if phase == 1:
            u = step
            for h in range(2):
                stage_2(u, h).wait_recv()
                total = (
                    partial[rows_of(u, h), columns_of(me)]
                    + recv_1[u, h, 0].astype(jnp.float32)
                    + recv_2[u, h].astype(jnp.float32)
                ) * scale
                diag[rows_of(u, h)] = total
                fock[rows_of(u, h), columns_of(me)] = total.astype(jnp.bfloat16)
            for axis in range(2):
                gather_1(u, axis).start()
            diag_copy(u).start()
        if phase == 2:
            u = step
            for axis in range(2):
                gather_1(u, 1 - axis).wait_recv()
                gather_2(u, axis).start()
        if phase == 3:
            u = step
            for axis in range(2):
                gather_2(u, axis).wait_recv()
            fock_copy(u).start()
    for g in range(groups):
        for i in order:
            @pl.when(jnp.logical_not(last_of[i // per_path]))
            def _():
                piece(g, i).wait_send()
    for u in range(units):
        for h in range(2):
            stage_1(u, h).wait_send()
            stage_2(u, h).wait_send()
            gather_1(u, h).wait_send()
            gather_2(u, h).wait_send()
        diag_copy(u).wait()
        fock_copy(u).wait()


def apply_kernel(
    listed, fock_in, density, diag_in, result, diag_out, fock, dens, out, diag,
    fock_sem, dens_sem, out_sem, diag_sem,
):
    rows, cols = density.shape
    groups = rows // W

    def fock_copy(g):
        part = pl.ds(g * W, W)
        return pltpu.make_async_copy(fock_in.at[part], fock.at[part], fock_sem.at[g])

    def dens_copy(t):
        part = pl.ds(t * TILE, TILE)
        return pltpu.make_async_copy(density.at[part], dens.at[part], dens_sem.at[t])

    def out_copy(m):
        part = pl.ds(m * BAND, BAND)
        return pltpu.make_async_copy(out.at[part], result.at[part], out_sem.at[m])

    for g in range(groups):
        for t in range(g * SUP, (g + 1) * SUP):
            dens_copy(t).start()
        fock_copy(g).start()
    pltpu.make_async_copy(diag_in, diag, diag_sem.at[0]).start()
    for g in range(groups):
        for t in range(g * SUP, (g + 1) * SUP):
            dens_copy(t).wait()
            part = pl.ds(t * TILE, TILE)
            for j in range(cols // TILE):
                span = pl.ds(j * TILE, TILE)
                dens[part, span] = mask_tile(dens[part, span], listed[t, j])
        fock_copy(g).wait()
        if g == 0:
            pltpu.make_async_copy(diag_in, diag, diag_sem.at[0]).wait()
            pltpu.make_async_copy(diag, diag_out, diag_sem.at[1]).start()
        for m in range(g * W // BAND, (g + 1) * W // BAND):
            part = pl.ds(m * BAND, BAND)
            product = jnp.dot(
                fock[part], dens[pl.ds(g * W, W)], preferred_element_type=jnp.float32
            )
            out[part] = (product * W ** (-0.5)).astype(jnp.bfloat16)
            out_copy(m).start()
    for m in range(rows // BAND):
        out_copy(m).wait()
    pltpu.make_async_copy(diag, diag_out, diag_sem.at[1]).wait()


def per_device_whole(density, listed, three_centre):
    rows, cols = density.shape
    groups = rows // W
    units = rows // UNIT
    aux_count = three_centre.shape[0]
    aux_group = aux_count * lax.axis_size("col") // groups
    bf16, dma = jnp.bfloat16, pltpu.SemaphoreType.DMA
    anywhere = pl.BlockSpec(memory_space=pl.ANY)
    diag, fock = pl.pallas_call(
        functools.partial(exchange_kernel, aux_group ** (-0.5)),
        out_shape=(
            jax.ShapeDtypeStruct((rows, TILE), jnp.float32),
            jax.ShapeDtypeStruct((rows, W), bf16),
        ),
        in_specs=[pl.BlockSpec(memory_space=pltpu.SMEM), anywhere, anywhere],
        out_specs=(anywhere, anywhere),
        scratch_shapes=[
            pltpu.VMEM((groups, W, W), bf16),
            pltpu.VMEM((groups, W, W), bf16),
            pltpu.VMEM((aux_count, W, W), bf16),
            pltpu.VMEM((aux_count // groups, W, W), bf16),
            pltpu.VMEM((rows, W), jnp.float32),
            pltpu.VMEM((units, 2, 2, PART, TILE), bf16),
            pltpu.VMEM((units, 2, 2, PART, TILE), bf16),
            pltpu.VMEM((units, 2, PART, TILE), bf16),
            pltpu.VMEM((units, 2, PART, TILE), bf16),
            pltpu.VMEM((rows, TILE), jnp.float32),
            pltpu.VMEM((rows, W), bf16),
            dma((groups,)),
            dma((aux_count,)),
            dma((units,)),
            dma((units,)),
            dma((groups, W // PIECE)),
            dma((groups, W // PIECE)),
        ]
        + [dma((units, 2)) for _ in range(8)],
        compiler_params=pltpu.CompilerParams(collective_id=0, has_side_effects=True),
    )(listed, density, three_centre)
    result, diag = pl.pallas_call(
        apply_kernel,
        out_shape=(
            jax.ShapeDtypeStruct((rows, cols), bf16),
            jax.ShapeDtypeStruct((rows, TILE), jnp.float32),
        ),
        in_specs=[pl.BlockSpec(memory_space=pltpu.SMEM), anywhere, anywhere, anywhere],
        out_specs=(anywhere, anywhere),
        scratch_shapes=[
            pltpu.VMEM((rows, W), bf16),
            pltpu.VMEM((rows, cols), bf16),
            pltpu.VMEM((rows, cols), bf16),
            pltpu.VMEM((rows, TILE), jnp.float32),
            dma((groups,)),
            dma((rows // TILE,)),
            dma((rows // BAND,)),
            dma((2,)),
        ],
    )(listed, fock, density, diag)
    return diag, result


def takes_whole(mesh, density, listed, three_centre):
    row_count, col_count = mesh.shape["row"], mesh.shape["col"]
    rows = density.shape[0] // row_count
    cols = density.shape[1] // col_count
    aux_count = three_centre.shape[0] // (row_count * col_count)
    if rows % W or cols % rows or col_count != 4 or col_count * TILE != W:
        return False
    return aux_count % (rows // W) == 0


def solution(mesh):
    placed = (P("row", "col"), P("row", "col"), P(("row", "col"), None, None))

    def mapped(body):
        return jax.shard_map(
            body,
            mesh=mesh,
            in_specs=placed,
            out_specs=(P("row", "col"), P("row", "col")),
            check_vma=False,
        )

    def run(density, listed, three_centre):
        whole = takes_whole(mesh, density, listed, three_centre)
        return mapped(per_device_whole if whole else per_device)(density, listed, three_centre)

    return run
```

profile of v0, /device:TPU:0, one launch (start us, length us, event | category | flops | bytes accessed | tf_op | source)
XLA Modules:
  0.0 51.1 jit_solution(2845896650031724481)
XLA Ops:
  0.6 42.7 %shard_map.50 = (f32[1024,128]{1,0:T(8,128)}, bf16[1024,512]{1,0:T(8,128)(2,1)}) custom-call(s32[8,16]{1,0:T(8,128)} %listed.3, bf16[1024,2048]{1,0:T(8,128)(2,1)} %density.3, bf16[4,512,512]{2,1,0:T(8,128)(2,1)} %three_centre.1), custom_call_target="tpu_custom_call" | custom-call | tf_op jit(solution)/shard_map/pallas_call | solution.py:367
  43.3 7.8 %shard_map.51 = (bf16[1024,2048]{1,0:T(8,128)(2,1)}, f32[1024,128]{1,0:T(8,128)}) custom-call(s32[8,16]{1,0:T(8,128)} %listed.3, bf16[1024,512]{1,0:T(8,128)(2,1)} %get-tuple-element.6.fock_in, bf16[1024,2048]{1,0:T(8,128)(2,1)} %density.3, f32[1024,128]{1,0:T(8,128)} %get-tuple-element.7.diag_in), custom_call_target="tpu_custom_call" | custom-call | tf_op jit(solution)/shard_map/pallas_call | solution.py:397
where the time goes:
time: 51.4 us; the launch traced here: 51.1 us
  Pallas kernels  50.5 us (98%)
  between operations  0.64 us (1%)
    pallas_call x1, Pallas kernels, per_device_whole(): pl.pallas_call(functools.partial(exchange_kernel, aux_group ** (-0.5)), o...  42.7 us
    pallas_call x1, Pallas kernels, per_device_whole(): pl.pallas_call(apply_kernel, out_shape=(jax.ShapeDtypeStruct((rows, cols)...  7.8 us

commit v1 on v0

v1 whole, which is shorter than its diff:
```python
import functools

import jax
import jax.numpy as jnp
from jax import lax
from jax.experimental import pallas as pl
from jax.experimental.pallas import tpu as pltpu
from jax.sharding import PartitionSpec as P

TILE = 128
W = 512
SUP = W // TILE
UNIT = W // 2
STRIP = W // 2
PART = UNIT // 2
PIECE = 64
HALF = W // 2
DIRECT = (0, 3)
BAND = 512
VMEM_GRANT = 32 * 2**20
MESH = pl.DeviceIdType.MESH


def from_root(value, axis, root):
    mine = lax.axis_index(axis) == root
    return lax.psum(jnp.where(mine, value, jnp.zeros_like(value)), axis)


def partner_2(block, axis, stride):
    count = lax.axis_size(axis)
    route = []
    for low in range(count):
        high = low | 1 << stride
        if high != low and high < count:
            route += [(low, high), (high, low)]
    return lax.ppermute(block, axis, route)


def halve_rows(values, row_index, levels, sender):
    for bit_level in reversed(range(levels)):
        middle = values.shape[0] // 2
        lower_half = row_index // 2**bit_level % 2 == 0
        kept_rows = jnp.where(lower_half, values[:middle], values[middle:])
        sent_rows = jnp.where(lower_half, values[middle:], values[:middle])
        values = kept_rows + sender(sent_rows, bit_level)
    return values


def per_device(density, listed, three_centre):
    tile_rows = listed.shape[0]
    tile_cols = listed.shape[1]
    quad_tiles = max(tile_rows, 4)
    groups_dev = quad_tiles // 4
    aux_count = three_centre.shape[0]
    col_count = lax.axis_size("col")
    row_index = lax.axis_index("row")
    col_index = lax.axis_index("col")
    masked = (
        density.reshape(tile_rows, TILE, tile_cols, TILE)
        * listed[:, None, :, None].astype(jnp.bfloat16)
    ).reshape(tile_rows * TILE, tile_cols * TILE)
    quad_start = row_index * tile_rows // quad_tiles * quad_tiles
    col_offset = quad_start % tile_cols * TILE
    portion = lax.dynamic_slice_in_dim(masked, col_offset, quad_tiles * TILE, 1)
    diagonal = from_root(portion, "col", quad_start // tile_cols)
    joined = jnp.concatenate([diagonal, masked], axis=1)
    levels = (quad_tiles // tile_rows).bit_length() - 1
    for bit_level in range(levels):
        partner = partner_2(joined, "row", bit_level)
        lower_half = row_index // 2**bit_level % 2 == 0
        joined = jnp.where(
            lower_half,
            jnp.concatenate([joined, partner], axis=0),
            jnp.concatenate([partner, joined], axis=0),
        )
    quad_block = joined[:, : quad_tiles * TILE]
    quad_density = joined[:, quad_tiles * TILE :]
    group_ids = jnp.arange(groups_dev, dtype=jnp.int32)
    exchange_quad = jnp.zeros((groups_dev, W, W), jnp.float32)
    for aux_slot in range(aux_count):
        group_slot = (col_index * aux_count + aux_slot) % groups_dev
        density_sub = lax.dynamic_slice(quad_block, (group_slot * W, group_slot * W), (W, W))
        aux_block = three_centre[aux_slot]
        half_product = jnp.dot(aux_block, density_sub, preferred_element_type=jnp.float32).astype(
            jnp.bfloat16
        )
        contribution = lax.dot_general(
            half_product, aux_block, (((1,), (1,)), ((), ())), preferred_element_type=jnp.float32
        )
        exchange_quad = exchange_quad + jnp.where(
            (group_ids == group_slot)[:, None, None], contribution[None], 0.0
        )
    aux_group = aux_count * col_count * 4 // tile_rows
    exchange_quad = (exchange_quad * aux_group ** (-0.5)).reshape(quad_tiles * TILE, W)
    column_share = lax.psum_scatter(exchange_quad, "col", scatter_dimension=1, tiled=True)
    exchange_diag = halve_rows(
        column_share,
        row_index,
        levels,
        lambda sent_rows, bit_level: partner_2(sent_rows, "row", bit_level),
    )
    fock_rounded = lax.all_gather(exchange_diag.astype(jnp.bfloat16), "col", axis=1, tiled=True)
    rows_here = tile_rows * TILE
    segment_rows = min(rows_here, W)
    segment_count = rows_here // segment_rows
    within_quad = (row_index * tile_rows - quad_start) * TILE
    products = []
    for segment in range(segment_count):
        group_position = (within_quad + segment * segment_rows) // W
        dens_rows = lax.dynamic_slice_in_dim(quad_density, group_position * W, W, 0)
        fock_part = fock_rounded[segment * segment_rows : (segment + 1) * segment_rows]
        products.append(
            jnp.dot(fock_part, dens_rows, preferred_element_type=jnp.float32) * W ** (-0.5)
        )
    exchange_density = jnp.concatenate(products, axis=0).astype(jnp.bfloat16)
    return (exchange_diag, exchange_density)


def mask_tile(tile, flag):
    return tile * jnp.full(tile.shape, flag.astype(jnp.float32)).astype(jnp.bfloat16)


def exchange_kernel(
    scale, listed, density, three_centre, early, masked_last, fock_last, diag,
    raw, block, coef, half, partial, send_1, recv_1, send_2, recv_2, fock, masked,
    raw_sem, coef_sem, dens_sem, bc_send, bc_recv, twin_send, rs1_send, rs1_recv,
    rs2_send, rs2_recv, ag1_send, ag1_recv, ag2_send, ag2_recv,
):
    tile_rows, tile_cols = listed.shape
    groups = tile_rows // SUP
    per_group = W // UNIT
    units = groups * per_group
    aux_count = three_centre.shape[0]
    row = lax.axis_index("row")
    me = lax.axis_index("col")
    x, y = me % 2, me // 2
    xn, yn = me + 1 - 2 * x, me + 2 - 4 * y
    far = xn + yn - me
    near = (xn, yn)
    first_tile = row * tile_rows
    owner = first_tile // tile_cols
    tile_off = first_tile % tile_cols
    ox, oy = owner % 2, owner // 2
    rx, ry = (x + ox) % 2, (y + oy) % 2
    even = (rx + ry + 1) % 2
    is_owner = rx + ry == 0
    is_far = rx + ry == 2
    hop_to = (xn * even + yn * (1 - even), yn * even + xn * (1 - even))
    last_of = (rx + 2 * (1 - ry) == 0, ry + 2 * (1 - rx) == 0)
    relays_of = (
        (rx + ry) * (rx + 1 - ry) > 0,
        (rx + ry) * (ry + 1 - rx) > 0,
    )
    lead = ry * (1 - rx)

    def remote(src, dst, send_sem, recv_sem, target):
        return pltpu.make_async_remote_copy(
            src_ref=src, dst_ref=dst, send_sem=send_sem, recv_sem=recv_sem,
            device_id=(row, target), device_id_type=MESH,
        )

    def raw_copy(g, p):
        start = (tile_off + g * SUP) * TILE + p * HALF
        columns = pl.ds(pl.multiple_of(start, TILE), HALF)
        return pltpu.make_async_copy(
            density.at[pl.ds(g * W, W), columns], raw.at[g, p], raw_sem.at[g, p]
        )

    def coef_copy(q):
        return pltpu.make_async_copy(three_centre.at[q], coef.at[q], coef_sem.at[q])

    def masked_of(g):
        return masked.at[g] if g < groups - 1 else masked_last

    def dens_copy(g):
        return pltpu.make_async_copy(
            density.at[pl.ds(g * W, W)], masked_of(g), dens_sem.at[g]
        )

    pieces = W // PIECE

    def piece(g, p, i):
        part = block.at[g, p, pl.ds(i * PIECE, PIECE)]
        return remote(part, part, bc_send.at[g, p, i], bc_recv.at[g, p, i], hop_to[p])

    def direct(g, i):
        return i >= pieces - (DIRECT[1] if g == groups - 1 else DIRECT[0]) * W // PIECE // 8

    def twin(g, p, i):
        part = block.at[g, p, pl.ds(i * PIECE, PIECE)]
        return remote(part, part, twin_send.at[g, p, i], bc_recv.at[g, p, i], hop_to[1 - p])

    @pl.when(is_owner)
    def _():
        for g in range(groups):
            for p in range(2):
                raw_copy(g, p).start()

    barrier = pltpu.get_barrier_semaphore()
    for neighbour in near:
        pl.semaphore_signal(barrier, inc=1, device_id=(row, neighbour), device_id_type=MESH)
    for q in range(aux_count):
        coef_copy(q).start()
    for g in range(groups):
        dens_copy(g).start()
    pl.semaphore_wait(barrier, 2)

    @pl.when(is_owner)
    def _():
        for g in range(groups):
            for p in range(2):
                raw_copy(g, p).wait()
            for i in range(pieces):
                rows = pl.ds(i * PIECE, PIECE)
                for p in range(2):
                    for j in range(HALF // TILE):
                        cols = pl.ds(j * TILE, TILE)
                        tile_col = tile_off + g * SUP + p * (HALF // TILE) + j
                        flag = listed[g * SUP + i * PIECE // TILE, tile_col]
                        block[g, p, rows, cols] = mask_tile(raw[g, p, rows, cols], flag)
                    piece(g, p, i).start()
                if direct(g, i):
                    for p in range(2):
                        twin(g, p, i).start()

    def sends(g, p, i):
        if direct(g, i):
            return relays_of[p] & jnp.logical_not(is_far)
        return relays_of[p]

    def relay(g, i):
        for p in range(2):
            @pl.when(sends(g, p, i))
            def _():
                piece(g, p, i).wait_recv()
                piece(g, p, i).start()

    def await_far(g):
        @pl.when(is_far)
        def _():
            for i in range(pieces):
                if direct(g, i):
                    for p in range(2):
                        piece(g, p, i).wait_recv()

    def await_last(g):
        for p in range(2):
            @pl.when(last_of[p])
            def _():
                for i in range(pieces):
                    piece(g, p, i).wait_recv()

    def stage_1(u, h):
        return remote(send_1.at[u, h], recv_1.at[u, h], rs1_send.at[u, h], rs1_recv.at[u, h], near[h])

    def stage_2(u, h):
        return remote(
            send_2.at[u, h], recv_2.at[u, h], rs2_send.at[u, h], rs2_recv.at[u, h], near[1 - h]
        )

    def columns_of(dev):
        return pl.ds(pl.multiple_of(dev * TILE, TILE), TILE)

    def rows_of(u, h):
        return pl.ds(u * UNIT + h * PART, PART)

    def fock_of(u):
        if u < units - per_group:
            return fock, u
        return fock_last, u - (units - per_group)

    def gather_1(u, axis):
        ref, v = fock_of(u)
        part = ref.at[pl.ds(v * UNIT, UNIT), columns_of(me)]
        return remote(part, part, ag1_send.at[u, axis], ag1_recv.at[u, axis], near[axis])

    def gather_2(u, axis):
        ref, v = fock_of(u)
        part = ref.at[rows_of(v, axis), columns_of(near[1 - axis])]
        return remote(part, part, ag2_send.at[u, axis], ag2_recv.at[u, axis], near[axis])

    def members(g):
        return list(range(g, aux_count, groups))

    def columns_half(p):
        return pl.ds(pl.multiple_of(p * HALF, HALF), HALF)

    def first_products(g, p):
        for n, q in enumerate(members(g)):
            yield lambda n=n, q=q: half.__setitem__(
                n, jnp.dot(coef[q], block[g, p], preferred_element_type=jnp.float32).astype(jnp.bfloat16)
            )

    def second_product(g, p, v, fresh):
        rows = pl.ds(v * STRIP, STRIP)
        total = None
        for n, q in enumerate(members(g)):
            term = lax.dot_general(
                half[n, rows], coef[q, :, columns_half(p)], (((1,), (1,)), ((), ())),
                preferred_element_type=jnp.float32,
            )
            total = term if total is None else total + term
        at = pl.ds(g * W + v * STRIP, STRIP)
        if fresh:
            partial[at] = total
        else:
            partial[at] += total

    def send_unit(u):
        for h in range(2):
            send_1[u, h, 0] = partial[rows_of(u, h), columns_of(near[h])].astype(jnp.bfloat16)
            send_1[u, h, 1] = partial[rows_of(u, h), columns_of(far)].astype(jnp.bfloat16)
            stage_1(u, h).start()

    def lead_work(g):
        yield from first_products(g, lead)
        for v in range(W // STRIP):
            yield lambda v=v: second_product(g, lead, v, True)

    def trail_work(g):
        yield from first_products(g, 1 - lead)
        for v in range(W // STRIP):
            def step(v=v):
                second_product(g, 1 - lead, v, False)
                for u in range(v * STRIP // UNIT, (v + 1) * STRIP // UNIT):
                    send_unit(g * per_group + u)
            yield step

    def mask_rows(g):
        for t in range(SUP):
            part = pl.ds(t * TILE, TILE)
            for j in range(tile_cols):
                span = pl.ds(j * TILE, TILE)
                ref = masked_of(g)
                ref[part, span] = mask_tile(ref[part, span], listed[g * SUP + t, j])

    for i in range(pieces):
        relay(0, i)
    for q in range(aux_count):
        coef_copy(q).wait()
    for g in range(groups):
        await_far(g)
        work = list(lead_work(g))
        if g + 1 < groups:
            for i in range(pieces):
                relay(g + 1, i)
                if i < len(work):
                    work[i]()
            work = work[pieces:]
        for step in work:
            step()
        if g + 1 == groups:
            for e in range(groups):
                dens_copy(e).wait()
                mask_rows(e)
        await_last(g)
        for step in trail_work(g):
            step()

    for phase, u in [(p, u) for p in range(4) for u in range(units)]:
        if phase == 0:
            for h in range(2):
                stage_1(u, h).wait_recv()
                send_2[u, h] = (
                    partial[rows_of(u, h), columns_of(near[1 - h])]
                    + recv_1[u, h, 1].astype(jnp.float32)
                ).astype(jnp.bfloat16)
                stage_2(u, h).start()
        if phase == 1:
            ref, v = fock_of(u)
            for h in range(2):
                stage_2(u, h).wait_recv()
                total = (
                    partial[rows_of(u, h), columns_of(me)]
                    + recv_1[u, h, 0].astype(jnp.float32)
                    + recv_2[u, h].astype(jnp.float32)
                ) * scale
                diag[rows_of(u, h)] = total
                ref[rows_of(v, h), columns_of(me)] = total.astype(jnp.bfloat16)
            for axis in range(2):
                gather_1(u, axis).start()
        if phase == 2:
            for axis in range(2):
                gather_1(u, 1 - axis).wait_recv()
                gather_2(u, axis).start()
        if phase == 3:
            for axis in range(2):
                gather_2(u, axis).wait_recv()
            g = u // per_group
            if u % per_group == per_group - 1 and g < groups - 1:
                apply_rows(fock.at[pl.ds(g * W, W)], masked.at[g], early, g * W)
    for g in range(groups):
        for i in range(pieces):
            for p in range(2):
                @pl.when(sends(g, p, i) | is_owner)
                def _():
                    piece(g, p, i).wait_send()
                if direct(g, i):
                    pl.when(is_owner)(twin(g, p, i).wait_send)
    for u in range(units):
        for h in range(2):
            stage_1(u, h).wait_send()
            stage_2(u, h).wait_send()
            gather_1(u, h).wait_send()
            gather_2(u, h).wait_send()


def apply_rows(fock, masked, out, start, after=None):
    for j in range(masked.shape[1] // BAND):
        span = pl.ds(j * BAND, BAND)
        product = jnp.dot(fock[...], masked[:, span], preferred_element_type=jnp.float32)
        out[pl.ds(start, W), span] = (product * W ** (-0.5)).astype(jnp.bfloat16)
        if after is not None:
            after(j)


def apply_kernel(early, masked, fock, diag, result, diag_out, out, early_sem, out_sem, diag_sem):
    ready = early.shape[0]
    early_copy = pltpu.make_async_copy(early, result.at[pl.ds(0, ready)], early_sem)
    diag_copy = pltpu.make_async_copy(diag, diag_out, diag_sem)

    def out_copy(j):
        span = pl.ds(j * BAND, BAND)
        return pltpu.make_async_copy(
            out.at[:, span], result.at[pl.ds(ready, W), span], out_sem.at[j]
        )

    early_copy.start()
    diag_copy.start()
    apply_rows(fock, masked, out, 0, lambda j: out_copy(j).start())
    for j in range(masked.shape[1] // BAND):
        out_copy(j).wait()
    early_copy.wait()
    diag_copy.wait()


def per_device_whole(density, listed, three_centre):
    rows, cols = density.shape
    groups = rows // W
    units = rows // UNIT
    aux_count = three_centre.shape[0]
    aux_group = aux_count * lax.axis_size("col") // groups
    bf16, dma = jnp.bfloat16, pltpu.SemaphoreType.DMA
    in_hbm = pl.BlockSpec(memory_space=pltpu.HBM)
    in_vmem = pl.BlockSpec(memory_space=pltpu.VMEM)
    handed = pl.pallas_call(
        functools.partial(exchange_kernel, aux_group ** (-0.5)),
        out_shape=(
            pltpu.VMEM((rows - W, cols), bf16),
            pltpu.VMEM((W, cols), bf16),
            pltpu.VMEM((W, W), bf16),
            pltpu.VMEM((rows, TILE), jnp.float32),
        ),
        in_specs=[pl.BlockSpec(memory_space=pltpu.SMEM), in_hbm, in_hbm],
        out_specs=(in_vmem,) * 4,
        scratch_shapes=[
            pltpu.VMEM((groups, 2, W, HALF), bf16),
            pltpu.VMEM((groups, 2, W, HALF), bf16),
            pltpu.VMEM((aux_count, W, W), bf16),
            pltpu.VMEM((aux_count // groups, W, HALF), bf16),
            pltpu.VMEM((rows, W), jnp.float32),
            pltpu.VMEM((units, 2, 2, PART, TILE), bf16),
            pltpu.VMEM((units, 2, 2, PART, TILE), bf16),
            pltpu.VMEM((units, 2, PART, TILE), bf16),
            pltpu.VMEM((units, 2, PART, TILE), bf16),
            pltpu.VMEM((rows - W, W), bf16),
            pltpu.VMEM((groups - 1, W, cols), bf16),
            dma((groups, 2)),
            dma((aux_count,)),
            dma((groups,)),
            dma((groups, 2, W // PIECE)),
            dma((groups, 2, W // PIECE)),
            dma((groups, 2, W // PIECE)),
        ]
        + [dma((units, 2)) for _ in range(8)],
        compiler_params=pltpu.CompilerParams(
            collective_id=0, has_side_effects=True, vmem_limit_bytes=VMEM_GRANT
        ),
    )(*(pltpu.with_memory_space_constraint(value, pltpu.HBM) for value in (listed, density, three_centre)))
    result, diag = pl.pallas_call(
        apply_kernel,
        out_shape=(
            jax.ShapeDtypeStruct((rows, cols), bf16),
            jax.ShapeDtypeStruct((rows, TILE), jnp.float32),
        ),
        in_specs=[in_vmem] * 4,
        out_specs=(in_hbm, in_hbm),
        scratch_shapes=[pltpu.VMEM((W, cols), bf16), dma, dma((cols // BAND,)), dma],
        compiler_params=pltpu.CompilerParams(vmem_limit_bytes=VMEM_GRANT),
    )(*(pltpu.with_memory_space_constraint(value, pltpu.VMEM) for value in handed))
    return diag, result


def takes_whole(mesh, density, listed, three_centre):
    row_count, col_count = mesh.shape["row"], mesh.shape["col"]
    rows = density.shape[0] // row_count
    cols = density.shape[1] // col_count
    aux_count = three_centre.shape[0] // (row_count * col_count)
    if rows % W or rows < 2 * W or cols % rows or col_count != 4 or col_count * TILE != W:
        return False
    return aux_count % (rows // W) == 0


def solution(mesh):
    placed = (P("row", "col"), P("row", "col"), P(("row", "col"), None, None))

    def mapped(body):
        return jax.shard_map(
            body,
            mesh=mesh,
            in_specs=placed,
            out_specs=(P("row", "col"), P("row", "col")),
            check_vma=False,
        )

    def run(density, listed, three_centre):
        whole = takes_whole(mesh, density, listed, three_centre)
        return mapped(per_device_whole if whole else per_device)(density, listed, three_centre)

    return run
```

time: 51.4 us -> 44.5 us (0.87)
  Pallas kernels: 50.5 us -> 43.7 us
    pallas_call x1, Pallas kernels: 7.8 us -> 2.23 us  [per_device_whole(): pl.pallas_call(apply_kernel, out_shape=(jax.ShapeDtypeStruct((rows, cols)...]
    pallas_call x1, Pallas kernels: 42.7 us -> 41.5 us  [per_device_whole(): pl.pallas_call(functools.partial(exchange_kernel, aux_group ** (-0.5)), o...]
where the time goes in v1:
time: 44.5 us; the launch traced here: 44.3 us
  Pallas kernels  43.7 us (98%)
  between operations  0.64 us (1%)
    pallas_call x1, Pallas kernels, per_device_whole(): pl.pallas_call(functools.partial(exchange_kernel, aux_group ** (-0.5)), o...  41.5 us
    pallas_call x1, Pallas kernels, per_device_whole(): pl.pallas_call(apply_kernel, out_shape=(jax.ShapeDtypeStruct((rows, cols)...  2.23 us

profile of v1, /device:TPU:0, one launch (start us, length us, event | category | flops | bytes accessed | tf_op | source)
XLA Modules:
  0.0 44.3 jit_solution(877441741311949361)
XLA Ops:
  0.6 41.5 %shard_map.50 = (bf16[512,2048]{1,0:T(8,128)(2,1)S(1)}, bf16[512,2048]{1,0:T(8,128)(2,1)S(1)}, bf16[512,512]{1,0:T(8,128)(2,1)S(1)}, f32[1024,128]{1,0:T(8,128)S(1)}) custom-call(s32[8,16]{1,0:T(8,128)} %listed.1, bf16[1024,2048]{1,0:T(8,128)(2,1)} %density.1, bf16[4,512,512]{2,1,0:T(8,128)(2,1)} %three_centre.1), custom_call_target="tpu_custom_call" | custom-call | tf_op jit(solution)/shard_map/pallas_call | solution.py:446
  42.1 2.2 %shard_map.51 = (bf16[1024,2048]{1,0:T(8,128)(2,1)}, f32[1024,128]{1,0:T(8,128)}) custom-call(bf16[512,2048]{1,0:T(8,128)(2,1)S(1)} %get-tuple-element.8.early, bf16[512,2048]{1,0:T(8,128)(2,1)S(1)} %get-tuple-element.9.masked, bf16[512,512]{1,0:T(8,128)(2,1)S(1)} %get-tuple-element.10.fock, f32[1024,128]{1,0:T(8,128)S(1)} %get-tuple-element.11.diag), custom_call_target="tpu_custom_call" | custom-call | tf_op jit(solution)/shard_map/pallas_call | solution.py:480

commit v2 on v1

--- a/solution.py
+++ b/solution.py
@@ -15,7 +15,7 @@
 PART = UNIT // 2
 PIECE = 64
 HALF = W // 2
-DIRECT = (0, 3)
+DIRECT = 3
 BAND = 512
 VMEM_GRANT = 32 * 2**20
 MESH = pl.DeviceIdType.MESH
@@ -163,11 +163,16 @@
         start = (tile_off + g * SUP) * TILE + p * HALF
         columns = pl.ds(pl.multiple_of(start, TILE), HALF)
         return pltpu.make_async_copy(
-            density.at[pl.ds(g * W, W), columns], raw.at[g, p], raw_sem.at[g, p]
-        )
-
-    def coef_copy(q):
-        return pltpu.make_async_copy(three_centre.at[q], coef.at[q], coef_sem.at[q])
+            density.at[pl.ds(g * W, W), columns], raw.at[g, p], raw_sem.at[g]
+        )
+
+    def filled(ref, sem):
+        pltpu.make_async_copy(ref, ref, sem).wait()
+
+    def sent(ref, sem):
+        remote(ref, ref, sem, sem, near[0]).wait_send()
+
+    coef_copy = pltpu.make_async_copy(three_centre, coef, coef_sem)
 
     def masked_of(g):
         return masked.at[g] if g < groups - 1 else masked_last
@@ -181,14 +186,17 @@
 
     def piece(g, p, i):
         part = block.at[g, p, pl.ds(i * PIECE, PIECE)]
-        return remote(part, part, bc_send.at[g, p, i], bc_recv.at[g, p, i], hop_to[p])
+        return remote(part, part, bc_send.at[g], bc_recv.at[g, p, i], hop_to[p])
+
+    def relayed(g):
+        return pieces - (DIRECT if g == groups - 1 else 0)
 
     def direct(g, i):
-        return i >= pieces - (DIRECT[1] if g == groups - 1 else DIRECT[0]) * W // PIECE // 8
+        return i >= relayed(g)
 
     def twin(g, p, i):
         part = block.at[g, p, pl.ds(i * PIECE, PIECE)]
-        return remote(part, part, twin_send.at[g, p, i], bc_recv.at[g, p, i], hop_to[1 - p])
+        return remote(part, part, twin_send.at[g], bc_recv.at[g, p, i], hop_to[1 - p])
 
     @pl.when(is_owner)
     def _():
@@ -199,8 +207,7 @@
     barrier = pltpu.get_barrier_semaphore()
     for neighbour in near:
         pl.semaphore_signal(barrier, inc=1, device_id=(row, neighbour), device_id_type=MESH)
-    for q in range(aux_count):
-        coef_copy(q).start()
+    coef_copy.start()
     for g in range(groups):
         dens_copy(g).start()
     pl.semaphore_wait(barrier, 2)
@@ -208,8 +215,7 @@
     @pl.when(is_owner)
     def _():
         for g in range(groups):
-            for p in range(2):
-                raw_copy(g, p).wait()
+            filled(raw.at[g], raw_sem.at[g])
             for i in range(pieces):
                 rows = pl.ds(i * PIECE, PIECE)
                 for p in range(2):
@@ -251,11 +257,11 @@
                     piece(g, p, i).wait_recv()
 
     def stage_1(u, h):
-        return remote(send_1.at[u, h], recv_1.at[u, h], rs1_send.at[u, h], rs1_recv.at[u, h], near[h])
+        return remote(send_1.at[u, h], recv_1.at[u, h], rs1_send, rs1_recv.at[u, h], near[h])
 
     def stage_2(u, h):
         return remote(
-            send_2.at[u, h], recv_2.at[u, h], rs2_send.at[u, h], rs2_recv.at[u, h], near[1 - h]
+            send_2.at[u, h], recv_2.at[u, h], rs2_send, rs2_recv.at[u, h], near[1 - h]
         )
 
     def columns_of(dev):
@@ -272,12 +278,12 @@
     def gather_1(u, axis):
         ref, v = fock_of(u)
         part = ref.at[pl.ds(v * UNIT, UNIT), columns_of(me)]
-        return remote(part, part, ag1_send.at[u, axis], ag1_recv.at[u, axis], near[axis])
+        return remote(part, part, ag1_send, ag1_recv.at[u, axis], near[axis])
 
     def gather_2(u, axis):
         ref, v = fock_of(u)
         part = ref.at[rows_of(v, axis), columns_of(near[1 - axis])]
-        return remote(part, part, ag2_send.at[u, axis], ag2_recv.at[u, axis], near[axis])
+        return remote(part, part, ag2_send, ag2_recv.at[u // per_group], near[axis])
 
     def members(g):
         return list(range(g, aux_count, groups))
@@ -334,10 +340,13 @@
                 ref = masked_of(g)
                 ref[part, span] = mask_tile(ref[part, span], listed[g * SUP + t, j])
 
+    def mask_all():
+        for g in range(groups):
+            mask_rows(g)
+
     for i in range(pieces):
         relay(0, i)
-    for q in range(aux_count):
-        coef_copy(q).wait()
+    coef_copy.wait()
     for g in range(groups):
         await_far(g)
         work = list(lead_work(g))
@@ -352,10 +361,11 @@
         if g + 1 == groups:
             for e in range(groups):
                 dens_copy(e).wait()
-                mask_rows(e)
+            pl.when(jnp.logical_not(is_far))(mask_all)
         await_last(g)
         for step in trail_work(g):
             step()
+    pl.when(is_far)(mask_all)
 
     for phase, u in [(p, u) for p in range(4) for u in range(units)]:
         if phase == 0:
@@ -384,25 +394,32 @@
                 gather_1(u, 1 - axis).wait_recv()
                 gather_2(u, axis).start()
         if phase == 3:
-            for axis in range(2):
-                gather_2(u, axis).wait_recv()
             g = u // per_group
-            if u % per_group == per_group - 1 and g < groups - 1:
+            if u % per_group < per_group - 1:
+                continue
+            whole = masked_of(g).at[:, pl.ds(0, TILE)]
+            remote(whole, whole, ag2_send, ag2_recv.at[g], near[0]).wait_recv()
+            if g < groups - 1:
                 apply_rows(fock.at[pl.ds(g * W, W)], masked.at[g], early, g * W)
     for g in range(groups):
-        for i in range(pieces):
-            for p in range(2):
-                @pl.when(sends(g, p, i) | is_owner)
-                def _():
-                    piece(g, p, i).wait_send()
-                if direct(g, i):
-                    pl.when(is_owner)(twin(g, p, i).wait_send)
-    for u in range(units):
-        for h in range(2):
-            stage_1(u, h).wait_send()
-            stage_2(u, h).wait_send()
-            gather_1(u, h).wait_send()
-            gather_2(u, h).wait_send()
+        @pl.when(is_owner)
+        def _():
+            sent(block.at[g], bc_send.at[g])
+            if relayed(g) < pieces:
+                tail = pl.ds(relayed(g) * PIECE, W - relayed(g) * PIECE)
+                sent(block.at[g, :, tail], twin_send.at[g])
+
+        @pl.when(is_far)
+        def _():
+            sent(block.at[g, :, pl.ds(0, relayed(g) * PIECE)], bc_send.at[g])
+
+        @pl.when(rx + ry == 1)
+        def _():
+            sent(block.at[g, 0], bc_send.at[g])
+    sent(send_1, rs1_send)
+    sent(send_2, rs2_send)
+    sent(send_1, ag1_send)
+    sent(send_1.at[:, 0], ag2_send)
 
 
 def apply_rows(fock, masked, out, start, after=None):
@@ -465,14 +482,21 @@
             pltpu.VMEM((units, 2, PART, TILE), bf16),
             pltpu.VMEM((rows - W, W), bf16),
             pltpu.VMEM((groups - 1, W, cols), bf16),
-            dma((groups, 2)),
-            dma((aux_count,)),
+            dma((groups,)),
+            dma,
+            dma((groups,)),
             dma((groups,)),
             dma((groups, 2, W // PIECE)),
-            dma((groups, 2, W // PIECE)),
-            dma((groups, 2, W // PIECE)),
-        ]
-        + [dma((units, 2)) for _ in range(8)],
+            dma((groups,)),
+            dma,
+            dma((units, 2)),
+            dma,
+            dma((units, 2)),
+            dma,
+            dma((units, 2)),
+            dma,
+            dma((groups,)),
+        ],
         compiler_params=pltpu.CompilerParams(
             collective_id=0, has_side_effects=True, vmem_limit_bytes=VMEM_GRANT
         ),

time: 44.5 us -> 42.6 us (0.957)
  Pallas kernels: 43.7 us -> 41.8 us
    pallas_call x1, Pallas kernels: 41.5 us -> 39.5 us  [per_device_whole(): pl.pallas_call(functools.partial(exchange_kernel, aux_group ** (-0.5)), o...]
where the time goes in v2:
time: 42.6 us; the launch traced here: 42.4 us
  Pallas kernels  41.8 us (98%)
  between operations  0.64 us (2%)
    pallas_call x1, Pallas kernels, per_device_whole(): pl.pallas_call(functools.partial(exchange_kernel, aux_group ** (-0.5)), o...  39.5 us
    pallas_call x1, Pallas kernels, per_device_whole(): pl.pallas_call(apply_kernel, out_shape=(jax.ShapeDtypeStruct((rows, cols)...  2.23 us

profile of v2, /device:TPU:0, one launch (start us, length us, event | category | flops | bytes accessed | tf_op | source)
XLA Modules:
  0.0 42.4 jit_solution(13282129339204428572)
XLA Ops:
  0.6 39.5 %shard_map.50 = (bf16[512,2048]{1,0:T(8,128)(2,1)S(1)}, bf16[512,2048]{1,0:T(8,128)(2,1)S(1)}, bf16[512,512]{1,0:T(8,128)(2,1)S(1)}, f32[1024,128]{1,0:T(8,128)S(1)}) custom-call(s32[8,16]{1,0:T(8,128)} %listed.1, bf16[1024,2048]{1,0:T(8,128)(2,1)} %density.1, bf16[4,512,512]{2,1,0:T(8,128)(2,1)} %three_centre.1), custom_call_target="tpu_custom_call" | custom-call | tf_op jit(solution)/shard_map/pallas_call | solution.py:463
  40.2 2.2 %shard_map.51 = (bf16[1024,2048]{1,0:T(8,128)(2,1)}, f32[1024,128]{1,0:T(8,128)}) custom-call(bf16[512,2048]{1,0:T(8,128)(2,1)S(1)} %get-tuple-element.8.early, bf16[512,2048]{1,0:T(8,128)(2,1)S(1)} %get-tuple-element.9.masked, bf16[512,512]{1,0:T(8,128)(2,1)S(1)} %get-tuple-element.10.fock, f32[1024,128]{1,0:T(8,128)S(1)} %get-tuple-element.11.diag), custom_call_target="tpu_custom_call" | custom-call | tf_op jit(solution)/shard_map/pallas_call | solution.py:504

commit v3 on v2

--- a/solution.py
+++ b/solution.py
@@ -15,6 +15,7 @@
 PART = UNIT // 2
 PIECE = 64
 HALF = W // 2
+OFFSET_NS = 7000
 DIRECT = 3
 BAND = 512
 VMEM_GRANT = 32 * 2**20
@@ -198,24 +199,26 @@
         part = block.at[g, p, pl.ds(i * PIECE, PIECE)]
         return remote(part, part, twin_send.at[g], bc_recv.at[g, p, i], hop_to[1 - p])
 
+    barrier = pltpu.get_barrier_semaphore()
+    for neighbour in near:
+        pl.semaphore_signal(barrier, inc=1, device_id=(row, neighbour), device_id_type=MESH)
+
     @pl.when(is_owner)
     def _():
         for g in range(groups):
             for p in range(2):
                 raw_copy(g, p).start()
 
-    barrier = pltpu.get_barrier_semaphore()
-    for neighbour in near:
-        pl.semaphore_signal(barrier, inc=1, device_id=(row, neighbour), device_id_type=MESH)
-    coef_copy.start()
-    for g in range(groups):
-        dens_copy(g).start()
     pl.semaphore_wait(barrier, 2)
 
     @pl.when(is_owner)
     def _():
         for g in range(groups):
             filled(raw.at[g], raw_sem.at[g])
+            if g == groups - 1:
+                @pl.when(row % 2 == 1)
+                def _():
+                    pl.delay(OFFSET_NS)
             for i in range(pieces):
                 rows = pl.ds(i * PIECE, PIECE)
                 for p in range(2):
@@ -344,6 +347,9 @@
         for g in range(groups):
             mask_rows(g)
 
+    coef_copy.start()
+    for g in range(groups):
+        dens_copy(g).start()
     for i in range(pieces):
         relay(0, i)
     coef_copy.wait()

time: 42.6 us -> 41.1 us (0.965)
  the two profiles are of different devices: /device:TPU:0 before, /device:TPU:1 now
where the time goes in v3:
time: 41.1 us; the launch traced here: 40.9 us
  Pallas kernels  40.3 us (98%)
  between operations  0.64 us (2%)
    pallas_call x1, Pallas kernels, per_device_whole(): pl.pallas_call(functools.partial(exchange_kernel, aux_group ** (-0.5)), o...  38 us
    pallas_call x1, Pallas kernels, per_device_whole(): pl.pallas_call(apply_kernel, out_shape=(jax.ShapeDtypeStruct((rows, cols)...  2.23 us

profile of v3, /device:TPU:1, one launch (start us, length us, event | category | flops | bytes accessed | tf_op | source)
XLA Modules:
  0.0 40.9 jit_solution(10057069754332427004)
XLA Ops:
  0.6 38.0 %shard_map.50 = (bf16[512,2048]{1,0:T(8,128)(2,1)S(1)}, bf16[512,2048]{1,0:T(8,128)(2,1)S(1)}, bf16[512,512]{1,0:T(8,128)(2,1)S(1)}, f32[1024,128]{1,0:T(8,128)S(1)}) custom-call(s32[8,16]{1,0:T(8,128)} %listed.1, bf16[1024,2048]{1,0:T(8,128)(2,1)} %density.1, bf16[4,512,512]{2,1,0:T(8,128)(2,1)} %three_centre.1), custom_call_target="tpu_custom_call" | custom-call | tf_op jit(solution)/shard_map/pallas_call | solution.py:469
  38.7 2.2 %shard_map.51 = (bf16[1024,2048]{1,0:T(8,128)(2,1)}, f32[1024,128]{1,0:T(8,128)}) custom-call(bf16[512,2048]{1,0:T(8,128)(2,1)S(1)} %get-tuple-element.8.early, bf16[512,2048]{1,0:T(8,128)(2,1)S(1)} %get-tuple-element.9.masked, bf16[512,512]{1,0:T(8,128)(2,1)S(1)} %get-tuple-element.10.fock, f32[1024,128]{1,0:T(8,128)S(1)} %get-tuple-element.11.diag), custom_call_target="tpu_custom_call" | custom-call | tf_op jit(solution)/shard_map/pallas_call | solution.py:510

commit v4 on v3

--- a/solution.py
+++ b/solution.py
@@ -327,9 +327,13 @@
             yield lambda v=v: second_product(g, lead, v, True)
 
     def trail_work(g):
-        yield from first_products(g, 1 - lead)
         for v in range(W // STRIP):
             def step(v=v):
+                rows = pl.ds(v * STRIP, STRIP)
+                for n, q in enumerate(members(g)):
+                    half[n, rows] = jnp.dot(
+                        coef[q, rows], block[g, 1 - lead], preferred_element_type=jnp.float32
+                    ).astype(jnp.bfloat16)
                 second_product(g, 1 - lead, v, False)
                 for u in range(v * STRIP // UNIT, (v + 1) * STRIP // UNIT):
                     send_unit(g * per_group + u)

time: 41.1 us -> 41.3 us (level)
  no operation moved by 1% of the time
where the time goes in v4:
time: 41.3 us; the launch traced here: 41.1 us
  Pallas kernels  40.5 us (98%)
  between operations  0.64 us (2%)
    pallas_call x1, Pallas kernels, per_device_whole(): pl.pallas_call(functools.partial(exchange_kernel, aux_group ** (-0.5)), o...  38.2 us
    pallas_call x1, Pallas kernels, per_device_whole(): pl.pallas_call(apply_kernel, out_shape=(jax.ShapeDtypeStruct((rows, cols)...  2.23 us

profile of v4, /device:TPU:1, one launch (start us, length us, event | category | flops | bytes accessed | tf_op | source)
XLA Modules:
  0.0 41.1 jit_solution(11587296074079727826)
XLA Ops:
  0.6 38.2 %shard_map.50 = (bf16[512,2048]{1,0:T(8,128)(2,1)S(1)}, bf16[512,2048]{1,0:T(8,128)(2,1)S(1)}, bf16[512,512]{1,0:T(8,128)(2,1)S(1)}, f32[1024,128]{1,0:T(8,128)S(1)}) custom-call(s32[8,16]{1,0:T(8,128)} %listed.1, bf16[1024,2048]{1,0:T(8,128)(2,1)} %density.1, bf16[4,512,512]{2,1,0:T(8,128)(2,1)} %three_centre.1), custom_call_target="tpu_custom_call" | custom-call | tf_op jit(solution)/shard_map/pallas_call | solution.py:473
  38.9 2.2 %shard_map.51 = (bf16[1024,2048]{1,0:T(8,128)(2,1)}, f32[1024,128]{1,0:T(8,128)}) custom-call(bf16[512,2048]{1,0:T(8,128)(2,1)S(1)} %get-tuple-element.8.early, bf16[512,2048]{1,0:T(8,128)(2,1)S(1)} %get-tuple-element.9.masked, bf16[512,512]{1,0:T(8,128)(2,1)S(1)} %get-tuple-element.10.fock, f32[1024,128]{1,0:T(8,128)S(1)} %get-tuple-element.11.diag), custom_call_target="tpu_custom_call" | custom-call | tf_op jit(solution)/shard_map/pallas_call | solution.py:514
